TPU v7x, 768 devices: a whole 4x8x12 slice. The times are simulated.
768 devices in a mesh: outer: 8 (over y), rep: 12 (over z_hi, x), mp: 8 (over z_lo, core).
Axes of the slice: x: 4, y: 8, z: 12 (z_hi: 3, z_lo: 4; z = z_hi * 4 + z_lo), core: 2. Of those that a mesh axis runs over, the one named last changes fastest.
Arguments:
- deltas: bfloat16 [8, 12, 768, 14336], P('outer', 'rep', None, 'mp'), may hold values from -6 to 6
- pod_momentum: float32 [8, 768, 14336], P('outer', 'rep', 'mp'), may hold values from -6 to 6
- global_momentum: float32 [12, 64, 14336], P('rep', 'outer', 'mp'), may hold values from -6 to 6
- master: float32 [12, 64, 14336], P('rep', 'outer', 'mp'), may hold values from -6 to 6
Outputs:
- params_new: bfloat16 [768, 14336], P(None, 'mp')
- pod_momentum_new: float32 [8, 768, 14336], P('outer', 'rep', 'mp')
- global_momentum_new: float32 [12, 64, 14336], P('rep', 'outer', 'mp')
All inputs are finite; a program needn't handle non-finite values.
Results may differ from a plain program's by a relative error of at most 0.011.
Values may be sent and summed in bfloat16 or wider, within the bound.
No kernel may reach another device: no remote copies, remote signals or barrier semaphores. Data moves between devices by JAX's collectives and lax.ppermute only.
A program may use at most 32 MiB of HBM per device.

v0:
```python
import jax
import jax.numpy as jnp
from jax import lax
from jax.sharding import Mesh
from jax.sharding import PartitionSpec as P

REP = ("rep_0", "rep_1")
OUTER_REP = ("outer", "rep_0", "rep_1")


def own_block(blocks, axes, turns):
    shape = [lax.axis_size(a) for a in axes]
    blocks = blocks.reshape(*shape, *blocks.shape[1:])
    blocks = blocks.transpose(*turns, *range(len(axes), blocks.ndim))
    blocks = blocks.reshape(-1, *blocks.shape[len(axes) :])
    for k in turns:
        blocks = lax.psum_scatter(blocks, axes[k], scatter_dimension=0, tiled=True)
    return blocks[0]


def cut_along(x, dim, devices):
    before, after = (x.shape[:dim], x.shape[dim + 1 :])
    return jnp.moveaxis(x.reshape(*before, devices, -1, *after), dim, 0)


def summed_rows(x, axes, turns, dim):
    devices = lax.axis_size(axes)
    return own_block(cut_along(x, dim, devices), axes, turns)


def sum_at_owner(x, axis, dim):
    devices = lax.axis_size(axis)
    blocks = lax.all_to_all(cut_along(x, dim, devices), axis, 0, 0, tiled=True)
    return jnp.sum(blocks.astype(jnp.float32), axis=0)


def in_order(blocks, dim):
    shape = list(blocks.shape[1:])
    shape[dim] *= blocks.shape[0]
    return jnp.moveaxis(blocks, 0, dim).reshape(shape)


def gather_in_order(x, axes, turns):
    blocks = x
    for k in turns:
        blocks = lax.all_gather(blocks, axes[k])
    done = turns[::-1]
    back = [done.index(k) for k in range(len(axes))]
    blocks = blocks.transpose(*back, *range(len(axes), blocks.ndim))
    return blocks.reshape(-1, *x.shape)


def gathered_by_axis(x, axes, turns, dim):
    return in_order(gather_in_order(x, axes, turns), dim)


def shards(deltas, pod_momentum, global_momentum, master):
    replicas = lax.axis_size(REP)
    pod_count = lax.axis_size("outer")
    own_delta = deltas[0, 0]
    pod_total = summed_rows(own_delta, REP, (1, 0), 0).astype(jnp.float32)
    pod_mean = pod_total / replicas
    pod_new = 0.9 * pod_momentum[0] + pod_mean
    pod_update = pod_mean + 0.9 * pod_new
    glob_total = sum_at_owner(pod_update.astype(jnp.bfloat16), "outer", 0)
    glob_mean = glob_total / pod_count
    glob_new = 0.8 * global_momentum[0] + glob_mean
    fresh = (master[0] - 0.7 * (glob_mean + 0.8 * glob_new)).astype(jnp.bfloat16)
    piece_rows = fresh.shape[0]
    columns = fresh.shape[1]
    gathered = gathered_by_axis(fresh[None], OUTER_REP, (1, 0, 2), 0)
    gathered = gathered.reshape(pod_count, replicas, piece_rows, columns)
    gathered = jnp.transpose(gathered, (1, 0, 2, 3)).reshape(
        replicas * pod_count * piece_rows, columns
    )
    return (gathered, pod_new[None], glob_new[None])


def solution(mesh):
    finer = Mesh(
        mesh.devices.reshape(mesh.shape["outer"], 3, 4, mesh.shape["mp"]),
        ("outer", "rep_0", "rep_1", "mp"),
    )
    return jax.shard_map(
        shards,
        mesh=finer,
        in_specs=(
            P("outer", REP, None, "mp"),
            P("outer", REP, "mp"),
            P(REP, "outer", "mp"),
            P(REP, "outer", "mp"),
        ),
        out_specs=(P(None, "mp"), P("outer", REP, "mp"), P(REP, "outer", "mp")),
        check_vma=False,
    )
```

profile of v0, /device:TPU:1, one launch (start us, length us, event | category | flops | bytes accessed | tf_op | source)
XLA Modules:
  0.0 218.2 jit_solution(6611787041060162876)
XLA Ops:
  7.2 0.0 reduce-scatter.3.cloned.1.call-start
  7.2 3.5 %copy.13 = bf16[3,4,64,1792]{3,2,0,1:T(8,128)(2,1)} copy(bf16[3,4,64,1792]{3,2,1,0:T(8,128)(2,1)} %bitcast.44) | data formatting | bytes 5505024 | tf_op jit(solution)/shard_map/reshape;reshape;squeeze | solution.py:13
  10.7 0.0 copy-start
  10.7 0.0 copy-start.2
  10.7 0.0 copy-start.3
  10.7 0.0 reduce-scatter.3.cloned.1.call-update
  10.8 0.0 reduce-scatter.5.cloned.1.call-start
  10.8 51.5 %reduce-scatter.3.cloned.1.call-done = bf16[3,64,1792]{2,1,0:T(8,128)(2,1)} async-done(((bf16[12,64,1792]{2,1,0:T(8,128)(2,1)}), bf16[3,64,1792]{2,1,0:T(8,128)(2,1)}) %reduce-scatter.3.cloned.1.call-update) | async-done | bytes 688144 | tf_op jit(solution)/shard_map/reduce_scatter | solution.py:17
  62.3 0.0 reduce-scatter.5.cloned.1.call-update
  62.3 0.0 all-gather.4.cloned.1.call-start
  62.4 45.2 %reduce-scatter.5.cloned.1.call-done = bf16[1,64,1792]{2,1,0:T(8,128)(2,1)} async-done(((bf16[3,64,1792]{2,1,0:T(8,128)(2,1)}), bf16[1,64,1792]{2,1,0:T(8,128)(2,1)}) %reduce-scatter.5.cloned.1.call-update) | async-done | bytes 229392 | tf_op jit(solution)/shard_map/reduce_scatter | solution.py:17
  107.6 0.0 copy-done
  107.6 0.0 copy-start.1
  107.6 1.1 fusion.2
  108.8 16.2 %all_to_all.5 = bf16[8,8,1792]{2,1,0:T(8,128)(2,1)S(1)} all-to-all(bf16[8,8,1792]{2,1,0:T(8,128)(2,1)S(1)} %fusion.2), channel_id=1, replica_groups=mesh['outer'=8,'rep_0'=3,'rep_1'=4,'mp'=8] {'outer'}, dimensions={0} | all-to-all | bytes 458752 | tf_op jit(solution)/shard_map/all_to_all | solution.py:33
  125.0 0.0 copy-done.2
  125.0 0.0 copy-done.3
  125.0 12.0 %all_gather.15 = bf16[3,1,8,1792]{3,2,1,0:T(8,128)(2,1)S(1)} all-gather(bf16[1,1,8,1792]{3,2,1,0:T(8,128)(2,1)S(1)} %fusion.8), channel_id=1, replica_groups=mesh['outer'=8,'rep_0'=3,'rep_1'=4,'mp'=8] {'rep_0'}, dimensions={0}, use_global_device_ids=true | all-gather | bytes 114688 | tf_op jit(solution)/shard_map/all_gather | solution.py:46
  137.0 22.4 %all-gather = bf16[24,1,8,1792]{3,2,1,0:T(8,128)(2,1)} all-gather(bf16[3,1,8,1792]{3,2,1,0:T(8,128)(2,1)S(1)} %all_gather.15), channel_id=2, replica_groups=mesh['outer'=8,'rep_0'=3,'rep_1'=4,'mp'=8] {'outer'}, dimensions={0}, use_global_device_ids=true | all-gather | bytes 774144 | tf_op jit(solution)/shard_map/all_gather | solution.py:46
  159.4 0.0 all-gather.4.cloned.1.call-update
  159.5 0.0 copy-done.1
  159.5 0.8 fusion.3
  160.3 0.6 bitcast_add_fusion.1
  160.9 46.9 %all-gather.4.cloned.1.call-done = bf16[32,3,1,8,1792]{4,3,2,1,0:T(8,128)(2,1)} async-done(((bf16[8,3,1,8,1792]{4,3,2,1,0:T(8,128)(2,1)}), bf16[32,3,1,8,1792]{4,3,2,1,0:T(8,128)(2,1)}) %all-gather.4.cloned.1.call-update) | async-done | bytes 2752528 | tf_op jit(solution)/shard_map/all_gather | solution.py:46
  207.8 2.1 copy.15
  209.9 1.8 copy.16
  (2 shorter events, 0.1 us)
Async XLA Ops:
  7.2 55.2 %reduce-scatter.3.cloned.1.call-start = ((), (), s32[]{:S(2)}) async-start(), calls=%async_computation.3 | async-start | bytes 3440640 | tf_op jit(solution)/shard_map/reduce_scatter | solution.py:17
  10.7 96.9 %copy-start = (f32[1,64,1792]{2,1,0:T(8,128)S(1)}, f32[1,64,1792]{2,1,0:T(8,128)}, u32[]{:S(2)}) copy-start(f32[1,64,1792]{2,1,0:T(8,128)} %param.5) | copy-start | bytes 1376260
  10.7 114.2 %copy-start.2 = (f32[1,8,1792]{2,1,0:T(8,128)S(1)}, f32[1,8,1792]{2,1,0:T(8,128)}, u32[]{:S(2)}) copy-start(f32[1,8,1792]{2,1,0:T(8,128)} %param.6) | copy-start | bytes 172036
  10.7 114.2 %copy-start.3 = (f32[1,8,1792]{2,1,0:T(8,128)S(1)}, f32[1,8,1792]{2,1,0:T(8,128)}, u32[]{:S(2)}) copy-start(f32[1,8,1792]{2,1,0:T(8,128)} %param.7) | copy-start | bytes 172036
  10.8 96.9 %reduce-scatter.5.cloned.1.call-start = ((), (), s32[]{:S(2)}) async-start(), calls=%async_computation.4 | async-start | bytes 917504 | tf_op jit(solution)/shard_map/reduce_scatter | solution.py:17
  62.3 145.4 %all-gather.4.cloned.1.call-start = ((), (), s32[]{:S(2)}) async-start(), calls=%async_computation.5 | async-start | bytes 3440640 | tf_op jit(solution)/shard_map/all_gather | solution.py:46
  107.6 51.8 %copy-start.1 = (bf16[1,64,1792]{2,1,0:T(8,128)(2,1)S(1)}, bf16[1,64,1792]{2,1,0:T(8,128)(2,1)}, u32[]{:S(2)}) copy-start(bf16[1,64,1792]{2,1,0:T(8,128)(2,1)} %reduce-scatter.5.cloned.1.call-done) | copy-start | bytes 688132
Sparse Core Ops, SparseCore 0:
  11.7 50.5 reduce-scatter.2
  65.5 42.1 reduce-scatter.4
  159.6 48.1 all-gather.3
where the time goes:
time: 218 us
  waiting for transfers between devices  144 us (66%)
  blocking collectives  50.6 us (23%)
  between operations  13.8 us (6%)
  local copies, waits for them, and re-layouts  7.42 us (3%)
  other arithmetic  2.64 us (1%)
    reduce_scatter x2, waiting for transfers between devices, own_block(): blocks = lax.psum_scatter(blocks, axes[k], scatter_dimension=0, tiled=True)  96.7 us
    all_gather x1, waiting for transfers between devices, gather_in_order(): blocks = lax.all_gather(blocks, axes[k])  46.9 us
    all_gather x2, blocking collectives, gather_in_order(): blocks = lax.all_gather(blocks, axes[k])  34.4 us
    all_to_all x1, blocking collectives, sum_at_owner(): blocks = lax.all_to_all(cut_along(x, dim, devices), axis, 0, 0, tiled=True)  16.2 us
  transfers between devices with their start and end apart: 3, of which 3 were waited for; matrix products, arithmetic and copies ran while one was open for 1% of the time, Pallas kernels for 0%

commit v1 on v0

v1 whole, which is shorter than its diff:
```python
import jax
import jax.numpy as jnp
from jax import lax
from jax.sharding import Mesh
from jax.sharding import PartitionSpec as P

REP = ("rep_0", "rep_1")


def exchange(blocks, axis):
    return lax.all_to_all(blocks, axis, 0, 0, tiled=True)


def total(blocks):
    return jnp.sum(blocks.astype(jnp.float32), axis=0)


def gathered(x, axis):
    return exchange(jnp.broadcast_to(x[None], (lax.axis_size(axis), *x.shape)), axis)


def shards(deltas, pod_momentum, global_momentum, master):
    n0, n1 = (lax.axis_size(a) for a in REP)
    pods = lax.axis_size("outer")
    replicas = n0 * n1
    columns = deltas.shape[-1]
    own = deltas[0, 0].reshape(n0, n1, -1, columns)
    by_x = exchange(jnp.swapaxes(own, 0, 1), "rep_1")
    by_z = exchange(total(by_x).astype(jnp.bfloat16), "rep_0")
    pod_mean = total(by_z) / replicas
    pod_new = 0.9 * pod_momentum[0] + pod_mean
    pod_update = (pod_mean + 0.9 * pod_new).astype(jnp.bfloat16)
    by_y = exchange(pod_update.reshape(pods, -1, columns), "outer")
    glob_mean = total(by_y) / pods
    glob_new = 0.8 * global_momentum[0] + glob_mean
    fresh = (master[0] - 0.7 * (glob_mean + 0.8 * glob_new)).astype(jnp.bfloat16)
    rows = gathered(gathered(fresh, "rep_0"), "outer")
    rows = gathered(jnp.swapaxes(rows, 0, 1), "rep_1")
    rows = jnp.swapaxes(rows, 0, 1).reshape(-1, columns)
    return (rows, pod_new[None], glob_new[None])


def solution(mesh):
    finer = Mesh(
        mesh.devices.reshape(mesh.shape["outer"], 3, 4, mesh.shape["mp"]),
        ("outer", "rep_0", "rep_1", "mp"),
    )
    return jax.shard_map(
        shards,
        mesh=finer,
        in_specs=(
            P("outer", REP, None, "mp"),
            P("outer", REP, "mp"),
            P(REP, "outer", "mp"),
            P(REP, "outer", "mp"),
        ),
        out_specs=(P(None, "mp"), P("outer", REP, "mp"), P(REP, "outer", "mp")),
        check_vma=False,
    )
```

time: 218 us -> 166 us (0.76)
  the two profiles are of different devices: /device:TPU:1 before, /device:TPU:192 now
where the time goes in v1:
time: 166 us; the launch traced here: 165 us
  blocking collectives  124 us (75%)
  waiting for transfers between devices  27.5 us (17%)
  local copies, waits for them, and re-layouts  5.59 us (3%)
  starting transfers between devices  3.67 us (2%)
  other arithmetic  3.49 us (2%)
    all_to_all x5, blocking collectives, exchange(): return lax.all_to_all(blocks, axis, 0, 0, tiled=True)  124 us
    all_to_all x1, waiting for transfers between devices, exchange(): return lax.all_to_all(blocks, axis, 0, 0, tiled=True)  27.5 us
    all_to_all x1, starting transfers between devices, exchange(): return lax.all_to_all(blocks, axis, 0, 0, tiled=True)  3.67 us
  transfers between devices with their start and end apart: 1, of which 1 were waited for; matrix products, arithmetic and copies ran while one was open for 1% of the time, Pallas kernels for 0%

profile of v1, /device:TPU:192, one launch (start us, length us, event | category | flops | bytes accessed | tf_op | source)
XLA Modules:
  0.0 165.4 jit_solution(14259814628250695215)
XLA Ops:
  0.6 2.0 %copy.11 = bf16[4,3,64,1792]{3,2,1,0:T(8,128)(2,1)S(1)} copy(bf16[4,3,64,1792]{3,2,0,1:T(8,128)(2,1)} %bitcast.33) | data formatting | bytes 5505024 | tf_op jit(solution)/shard_map/transpose | solution.py:28
  2.6 37.4 %all_to_all.30 = bf16[4,3,64,1792]{3,2,1,0:T(8,128)(2,1)S(1)} all-to-all(bf16[4,3,64,1792]{3,2,1,0:T(8,128)(2,1)S(1)} %copy.11), channel_id=1, replica_groups=mesh['outer'=8,'rep_0'=3,'rep_1'=4,'mp'=8] {'rep_1'}, dimensions={0} | all-to-all | bytes 5505024 | tf_op jit(solution)/shard_map/all_to_all | solution.py:11
  40.0 0.8 reduce_sum.30
  40.8 0.0 copy-start
  40.8 0.0 copy-start.1
  40.8 0.0 copy-start.2
  40.8 35.9 %all_to_all.31 = bf16[3,64,1792]{2,1,0:T(8,128)(2,1)S(1)} all-to-all(bf16[3,64,1792]{2,1,0:T(8,128)(2,1)S(1)} %reduce_sum.30), channel_id=1, replica_groups=mesh['outer'=8,'rep_0'=3,'rep_1'=4,'mp'=8] {'rep_0'}, dimensions={0} | all-to-all | bytes 1376256 | tf_op jit(solution)/shard_map/all_to_all | solution.py:11
  76.8 0.1 convert_reduce_fusion
  76.9 0.0 copy-done
  76.9 0.1 fusion.2
  77.0 18.3 %all_to_all.32 = bf16[8,8,1792]{2,1,0:T(8,128)(2,1)S(1)} all-to-all(bf16[8,8,1792]{2,1,0:T(8,128)(2,1)S(1)} %fusion.2), channel_id=1, replica_groups=mesh['outer'=8,'rep_0'=3,'rep_1'=4,'mp'=8] {'outer'}, dimensions={0} | all-to-all | bytes 458752 | tf_op jit(solution)/shard_map/all_to_all | solution.py:11
  95.3 0.0 copy-done.1
  95.3 0.0 copy-done.2
  95.3 0.6 fusion.6
  95.9 11.9 %all_to_all.33 = bf16[3,8,1792]{2,1,0:T(8,128)(2,1)S(1)} all-to-all(bf16[3,8,1792]{2,1,0:T(8,128)(2,1)S(1)} %broadcast_in_dim.9), channel_id=1, replica_groups=mesh['outer'=8,'rep_0'=3,'rep_1'=4,'mp'=8] {'rep_0'}, dimensions={0} | all-to-all | bytes 172032 | tf_op jit(solution)/shard_map/all_to_all | solution.py:11
  107.9 20.9 %all_to_all.34 = bf16[8,3,8,1792]{3,2,1,0:T(8,128)(2,1)S(1)} all-to-all(bf16[8,3,8,1792]{3,2,1,0:T(8,128)(2,1)S(1)} %broadcast_in_dim.10), channel_id=1, replica_groups=mesh['outer'=8,'rep_0'=3,'rep_1'=4,'mp'=8] {'outer'}, dimensions={0} | all-to-all | bytes 1376256 | tf_op jit(solution)/shard_map/all_to_all | solution.py:11
  128.8 1.8 %broadcast_in_dim.11 = bf16[4,3,8,8,1792]{4,3,2,1,0:T(8,128)(2,1)} broadcast(bf16[3,8,8,1792]{3,2,1,0:T(8,128)(2,1)S(1)} %copy.12), dimensions={1,2,3,4} | broadcast | bytes 3440640 | tf_op jit(solution)/shard_map/broadcast_in_dim | solution.py:19
  130.6 3.7 %all-to-all-start.5 = ((bf16[4,3,8,8,1792]{4,3,2,1,0:T(8,128)(2,1)}), bf16[4,3,8,8,1792]{4,3,2,1,0:T(8,128)(2,1)S(1)}, u32[]{:S(2)}, u32[]{:S(2)}) async-start(bf16[4,3,8,8,1792]{4,3,2,1,0:T(8,128)(2,1)} %broadcast_in_dim.11), calls=%async_computation.5 | async-start | bytes 5505024 | tf_op jit(solution)/shard_map/all_to_all | solution.py:11
  134.3 1.9 %bitcast_add_fusion = f32[1,64,1792]{2,1,0:T(8,128)} fusion(f32[1,64,1792]{2,1,0:T(8,128)} %param.5, f32[64,1792]{1,0:T(8,128)S(1)} %convert_reduce_fusion), kind=kLoop, calls=%fused_computation.1 | loop fusion | flops 344064 | bytes 1376256 | tf_op jit(solution)/shard_map/add | solution.py:31
  136.1 27.5 %all-to-all-done.5 = bf16[4,3,8,8,1792]{4,3,2,1,0:T(8,128)(2,1)S(1)} async-done(((bf16[4,3,8,8,1792]{4,3,2,1,0:T(8,128)(2,1)}), bf16[4,3,8,8,1792]{4,3,2,1,0:T(8,128)(2,1)S(1)}, u32[]{:S(2)}, u32[]{:S(2)}) %all-to-all-start.5) | async-done | bytes 2752544 | tf_op jit(solution)/shard_map/all_to_all | solution.py:11
  163.6 1.7 %copy.13 = bf16[4,3,8,8,1792]{4,3,2,0,1:T(8,128)(2,1)} copy(bf16[4,3,8,8,1792]{4,3,2,1,0:T(8,128)(2,1)S(1)} %all-to-all-done.5) | data formatting | bytes 5505024 | tf_op jit(solution)/shard_map/all_to_all | solution.py:11
  (4 shorter events, 0.1 us)
Async XLA Ops:
  40.8 36.0 %copy-start = (f32[1,64,1792]{2,1,0:T(8,128)S(1)}, f32[1,64,1792]{2,1,0:T(8,128)}, u32[]{:S(2)}) copy-start(f32[1,64,1792]{2,1,0:T(8,128)} %param.5) | copy-start | bytes 1376260
  40.8 54.4 %copy-start.1 = (f32[1,8,1792]{2,1,0:T(8,128)S(1)}, f32[1,8,1792]{2,1,0:T(8,128)}, u32[]{:S(2)}) copy-start(f32[1,8,1792]{2,1,0:T(8,128)} %param.7) | copy-start | bytes 172036
  40.8 54.4 %copy-start.2 = (f32[1,8,1792]{2,1,0:T(8,128)S(1)}, f32[1,8,1792]{2,1,0:T(8,128)}, u32[]{:S(2)}) copy-start(f32[1,8,1792]{2,1,0:T(8,128)} %param.6) | copy-start | bytes 172036
  130.6 33.0 %all-to-all-start.5 = ((bf16[4,3,8,8,1792]{4,3,2,1,0:T(8,128)(2,1)}), bf16[4,3,8,8,1792]{4,3,2,1,0:T(8,128)(2,1)S(1)}, u32[]{:S(2)}, u32[]{:S(2)}) async-start(bf16[4,3,8,8,1792]{4,3,2,1,0:T(8,128)(2,1)} %broadcast_in_dim.11), calls=%async_computation.5 | async-start | bytes 5505024 | tf_op jit(solution)/shard_map/all_to_all | solution.py:11
